TPU v7x, 256 devices: a whole 4x4x8 slice. The times are simulated.
256 devices in a mesh: tier: 8 (over y, core), mode: 32 (over x, z).
Axes of the slice: x: 4, y: 4, z: 8, core: 2. Of those that a mesh axis runs over, the one named last changes fastest.
Arguments:
- ados: float32 [8, 32, 2, 2, 9216], P('tier', 'mode'), may hold values from -6 to 6
- hamiltonian: float32 [96, 96], replicated, may hold values from -0.3125 to 0.3125
- couplings: float32 [16, 96], replicated, may hold values from -2.4 to 2.4
- rates: float32 [16], replicated, may hold values from 0.05 to 0.6
- strength: float32 [2, 16], replicated, may hold values from -1.8 to 1.8
- occupancy: int32 [8, 32, 2, 16], P('tier', 'mode'), may hold values from 0 to 8, as said below
- up_index: int32 [8, 32, 2, 16], P('tier', 'mode'), may hold values from 0 to 8, as said below
- down_index: int32 [8, 32, 2, 16], P('tier', 'mode'), may hold values from 0 to 8, as said below
Outputs:
- evolved: float32 [8, 32, 2, 2, 9216], P('tier', 'mode')
Inputs may be any that keep to these rules, and one draw needn't show every extreme that they name: `occupancy`: each matrix is occupied in at most 8 quanta in all, summed over the 16 modes; higher tier bins hold matrices of higher tiers on average. For each mode, up_index and down_index describe the same pairs in the two directions: if the entry of matrix a for mode k in up_index names matrix b, then the entry of b for mode k in down_index names a, and the reverse; no matrix is named twice for one mode. The value 4 * 2 names no matrix, and no entry names a tier outside the hierarchy. `down_index`: see up_index.
All inputs are finite; a program needn't handle non-finite values.
Results may differ from a plain program's by a relative error of at most 0.00005.
Values sent between devices are 32-bit elements; how exact they have to be, the bound alone decides.
A program may use at most 64 MiB of HBM per device.

v0:
```python
import jax
import jax.numpy as jnp
from jax import lax
from jax.experimental import pallas as pl
from jax.experimental.pallas import tpu as pltpu
from jax.sharding import PartitionSpec as P

TIME_STEP = 0.3
STAGES = 4
HIGHEST = lax.Precision.HIGHEST
MESH_ID = pl.DeviceIdType.MESH

LOWER_TIER, UPPER_TIER, LOWER_MODE, UPPER_MODE, LOWER_DIAG, UPPER_DIAG = range(6)
PIECES = 3
GROUPS = 24


def lane_index():
    return lax.broadcasted_iota(jnp.int32, (GROUPS, 128), 1)


def widen(row):
    lane = lax.broadcasted_iota(jnp.int32, row.shape, 1)
    by96, by64, by32 = (pltpu.roll(row, shift, 1) for shift in (96, 64, 32))
    return (
        jnp.where(lane < 96, row, by96),
        jnp.where(lane < 64, by96, by64),
        jnp.where(lane < 32, by64, by32),
    )


def unpack(pieces):
    lane = lane_index()
    first, second, third = pieces
    return jnp.concatenate(
        [
            first,
            jnp.where(lane < 32, pltpu.roll(first, 32, 1), pltpu.roll(second, 32, 1)),
            jnp.where(lane < 64, pltpu.roll(second, 64, 1), pltpu.roll(third, 64, 1)),
            pltpu.roll(third, 96, 1),
        ],
        axis=0,
    )


def pack(rows):
    lane = lane_index()
    part = [rows[GROUPS * p : GROUPS * (p + 1)] for p in range(4)]
    one96, two64 = pltpu.roll(part[1], 96, 1), pltpu.roll(part[2], 64, 1)
    return (
        jnp.where(lane < 96, part[0], one96),
        jnp.where(lane < 64, one96, two64),
        jnp.where(lane < 32, two64, pltpu.roll(part[3], 32, 1)),
    )


def kernel(
    a_ref, ham_ref, cpl_ref, rates_ref, strength_ref, occ_ref, up_ref, down_ref,
    out_ref,
    own, halo, acc, gap_up, gap_down, plus_down, ham_sq, ham_perm, tall, send_sem, recv_sem,
):
    tier, mode = lax.axis_index("tier"), lax.axis_index("mode")
    tiers, modes = lax.axis_size("tier"), lax.axis_size("mode")
    next_mode, prev_mode = lax.rem(mode + 1, modes), lax.rem(mode + modes - 1, modes)
    has_lower, has_upper = tier > 0, tier < tiers - 1

    barrier = pltpu.get_barrier_semaphore()

    def greet(device):
        pl.semaphore_signal(barrier, inc=1, device_id=device, device_id_type=MESH_ID)

    greet((tier, next_mode))
    greet((tier, prev_mode))

    @pl.when(has_upper)
    def _():
        greet((tier + 1, mode))

    @pl.when(has_lower)
    def _():
        greet((tier - 1, mode))

    for s in range(2):
        for ri in range(2):
            for u in range(PIECES):
                own[0, u, 2 * s + ri] = a_ref[s, pl.ds(2 * u + ri, GROUPS, stride=6), :]

    blank = jnp.zeros((4, GROUPS, 128), jnp.float32)

    @pl.when(jnp.logical_not(has_lower))
    def _():
        for n in range(STAGES):
            for u in range(PIECES):
                halo[n, LOWER_TIER, u] = blank
                halo[n, LOWER_DIAG, u] = blank

    @pl.when(jnp.logical_not(has_upper))
    def _():
        for n in range(STAGES):
            for u in range(PIECES):
                halo[n, UPPER_TIER, u] = blank
                halo[n, UPPER_DIAG, u] = blank

    @pl.when(jnp.logical_and(has_upper, has_lower))
    def _():
        pl.semaphore_wait(barrier, 4)

    @pl.when(jnp.logical_not(jnp.logical_and(has_upper, has_lower)))
    def _():
        pl.semaphore_wait(barrier, 3)

    def copy(n, slot, u, src, device):
        return pltpu.make_async_remote_copy(
            src_ref=src,
            dst_ref=halo.at[n, slot, u],
            send_sem=send_sem.at[n, slot, u],
            recv_sem=recv_sem.at[n, slot, u],
            device_id=device,
            device_id_type=MESH_ID,
        )

    def copies(n, slot, u):
        source = {
            LOWER_DIAG: halo.at[n, LOWER_MODE, u],
            UPPER_DIAG: halo.at[n, UPPER_MODE, u],
        }.get(slot, own.at[n, u])
        device = {
            LOWER_TIER: (tier + 1, mode),
            LOWER_DIAG: (tier + 1, mode),
            UPPER_TIER: (tier - 1, mode),
            UPPER_DIAG: (tier - 1, mode),
            LOWER_MODE: (tier, next_mode),
            UPPER_MODE: (tier, prev_mode),
        }[slot]
        return copy(n, slot, u, source, device)

    sends_if = {
        LOWER_TIER: has_upper, LOWER_DIAG: has_upper,
        UPPER_TIER: has_lower, UPPER_DIAG: has_lower,
        LOWER_MODE: None, UPPER_MODE: None,
    }
    comes_if = {
        LOWER_TIER: has_lower, LOWER_DIAG: has_lower,
        UPPER_TIER: has_upper, UPPER_DIAG: has_upper,
        LOWER_MODE: None, UPPER_MODE: None,
    }

    def when(condition, act):
        if condition is None:
            act()
        else:
            pl.when(condition)(act)

    def start(n, slot, u):
        when(sends_if[slot], lambda: copies(n, slot, u).start())

    def arrive(n, slot, u):
        when(comes_if[slot], lambda: copies(n, slot, u).wait_recv())

    def send_own(n, u):
        for slot in (LOWER_MODE, UPPER_MODE, LOWER_TIER, UPPER_TIER):
            start(n, slot, u)

    for u in range(PIECES):
        send_own(0, u)

    raw = ham_ref[...]
    ham_sq[...] = jnp.zeros((128, 128), jnp.float32)
    ham_sq[:96, :96] = 0.5 * (raw + raw.T)
    rows = jnp.concatenate([ham_sq[pl.ds(p, GROUPS, stride=4), :] for p in range(4)], axis=0)
    tall[...] = jnp.concatenate([rows, jnp.zeros((32, 128), jnp.float32)], axis=0).T
    ham_perm[...] = jnp.concatenate([tall[pl.ds(p, GROUPS, stride=4), :] for p in range(4)], axis=0)

    level = occ_ref[...].astype(jnp.float32)
    named = lax.broadcasted_iota(jnp.int32, (8, 16), 0)
    ups, down_re, down_im = [], [], []
    for s in range(2):
        up_mask = (up_ref[s : s + 1, :] == named).astype(jnp.float32)
        down_mask = (down_ref[s : s + 1, :] == named).astype(jnp.float32) * level[s : s + 1, :]
        ups.append(up_mask)
        down_re.append(down_mask * strength_ref[0:1, :])
        down_im.append(down_mask * strength_ref[1:2, :])
    own_rows = lax.broadcasted_iota(jnp.int32, (8, 16), 0) < 2
    down_re = [d + jnp.where(own_rows, v, 0.0) for d, v in zip(down_re, ups)]
    mix = jnp.concatenate(ups + down_re + down_im, axis=0)
    cpl = cpl_ref[...]
    wide_cpl = jnp.concatenate([cpl, jnp.zeros((16, 32), jnp.float32)], axis=1)
    by_lane = jnp.dot(mix, wide_cpl, precision=HIGHEST, preferred_element_type=jnp.float32)
    flat = lax.dot_general(
        wide_cpl, mix, (((0,), (1,)), ((), ())), precision=HIGHEST, preferred_element_type=jnp.float32
    )
    tall[:, :48] = flat
    columns = [tall[pl.ds(p, GROUPS, stride=4), :] for p in range(4)]
    lane = lane_index()
    lanes_wide = widen(by_lane)
    damping = jnp.sum(level * rates_ref[...], axis=1, keepdims=True)
    for e in range(48):
        kind, s, source = e // 16, e // 8 % 2, e % 8
        if kind == 0 and source < 2:
            continue
        spread = [jnp.broadcast_to(columns[p][:, e : e + 1], (GROUPS, 128)) for p in range(4)]
        for u in range(PIECES):
            along_rows = jnp.where(lane < (96, 64, 32)[u], spread[u], spread[u + 1])
            along_lanes = lanes_wide[u][e : e + 1, :]
            if kind == 0:
                gap_up[8 * s + source, u] = along_rows - along_lanes
            elif kind == 1:
                gap_down[8 * s + source, u] = along_rows - along_lanes
            else:
                plus = along_rows + along_lanes
                if source == s:
                    plus = plus - damping[s : s + 1, :]
                plus_down[8 * s + source, u] = plus

    def add_up(sums, src, block, u):
        for j in range(2):
            real, imag = src[2 * j], src[2 * j + 1]
            for s in range(2):
                gap = gap_up[8 * s + 2 * block + j, u]
                sums[2 * s] = sums[2 * s] + gap * imag
                sums[2 * s + 1] = sums[2 * s + 1] - gap * real

    def add_down(sums, src, block, u):
        for j in range(2):
            real, imag = src[2 * j], src[2 * j + 1]
            for s in range(2):
                gap, plus = gap_down[8 * s + 2 * block + j, u], plus_down[8 * s + 2 * block + j, u]
                sums[2 * s] = sums[2 * s] + gap * imag + plus * real
                sums[2 * s + 1] = sums[2 * s + 1] + plus * imag - gap * real

    for n in range(STAGES):
        whole = [unpack([own[n, u, c] for u in range(PIECES)]) for c in range(4)]
        right = jnp.dot(
            jnp.concatenate(whole, axis=0), ham_sq[...], precision=HIGHEST, preferred_element_type=jnp.float32
        )
        left = jnp.dot(
            ham_perm[:, :96], jnp.concatenate(whole, axis=1), precision=HIGHEST, preferred_element_type=jnp.float32
        )
        moved = [pack(left[:, 128 * c : 128 * (c + 1)] - right[96 * c : 96 * (c + 1)]) for c in range(4)]
        for u in range(PIECES):
            sums = [moved[1][u], -moved[0][u], moved[3][u], -moved[2][u]]
            add_down(sums, own.at[n, u], 0, u)
            for c in range(4):
                acc[u, c] = sums[c]

        for u in range(PIECES):
            arrive(n, LOWER_MODE, u)
            start(n, LOWER_DIAG, u)
            arrive(n, UPPER_MODE, u)
            start(n, UPPER_DIAG, u)
            arrive(n, LOWER_TIER, u)
            arrive(n, UPPER_TIER, u)
            sums = [acc[u, c] for c in range(4)]
            add_down(sums, halo.at[n, LOWER_MODE, u], 2, u)
            add_up(sums, halo.at[n, UPPER_MODE, u], 2, u)
            add_down(sums, halo.at[n, LOWER_TIER, u], 1, u)
            add_up(sums, halo.at[n, UPPER_TIER, u], 1, u)
            for c in range(4):
                acc[u, c] = sums[c]

        for u in range(PIECES):
            arrive(n, LOWER_DIAG, u)
            arrive(n, UPPER_DIAG, u)
            sums = [acc[u, c] for c in range(4)]
            add_down(sums, halo.at[n, LOWER_DIAG, u], 3, u)
            add_up(sums, halo.at[n, UPPER_DIAG, u], 3, u)
            for c in range(4):
                term = (TIME_STEP / (n + 1)) * sums[c]
                if n < STAGES - 1:
                    own[n + 1, u, c] = term
                else:
                    total = term
                    for back in range(STAGES - 1, -1, -1):
                        total = total + own[back, u, c]
                    out_ref[c // 2, pl.ds(2 * u + c % 2, GROUPS, stride=6), :] = total
            if n < STAGES - 1:
                send_own(n + 1, u)

    for n in range(STAGES):
        for u in range(PIECES):
            for slot in range(6):
                when(sends_if[slot], lambda n=n, slot=slot, u=u: copies(n, slot, u).wait_send())


def shards(ados, hamiltonian, couplings, rates, strength, occupancy, up_index, down_index):
    rows = ados.reshape(2, 2, 72, 128).transpose(0, 2, 1, 3).reshape(2, 144, 128)
    vmem = pl.BlockSpec(memory_space=pltpu.VMEM)
    done = pl.pallas_call(
        kernel,
        out_shape=jax.ShapeDtypeStruct((2, 144, 128), jnp.float32),
        in_specs=[vmem] * 8,
        out_specs=vmem,
        scratch_shapes=[
            pltpu.VMEM((STAGES, PIECES, 4, GROUPS, 128), jnp.float32),
            pltpu.VMEM((STAGES, 6, PIECES, 4, GROUPS, 128), jnp.float32),
            pltpu.VMEM((PIECES, 4, GROUPS, 128), jnp.float32),
            pltpu.VMEM((16, PIECES, GROUPS, 128), jnp.float32),
            pltpu.VMEM((16, PIECES, GROUPS, 128), jnp.float32),
            pltpu.VMEM((16, PIECES, GROUPS, 128), jnp.float32),
            pltpu.VMEM((128, 128), jnp.float32),
            pltpu.VMEM((96, 128), jnp.float32),
            pltpu.VMEM((128, 128), jnp.float32),
            pltpu.SemaphoreType.DMA((STAGES, 6, PIECES)),
            pltpu.SemaphoreType.DMA((STAGES, 6, PIECES)),
        ],
        compiler_params=pltpu.CompilerParams(collective_id=0, has_side_effects=True),
    )(
        rows, hamiltonian, couplings, rates.reshape(1, -1), strength,
        occupancy.reshape(2, -1), up_index.reshape(2, -1), down_index.reshape(2, -1),
    )
    return done.reshape(2, 72, 2, 128).transpose(0, 2, 1, 3).reshape(ados.shape)


def solution(mesh):
    split = P("tier", "mode", None, None)
    in_specs = (P("tier", "mode", None, None, None), P(), P(), P(), P(), split, split, split)
    out_specs = P("tier", "mode", None, None, None)
    return jax.shard_map(shards, mesh=mesh, in_specs=in_specs, out_specs=out_specs, check_vma=False)
```

profile of v0, /device:TPU:1, one launch (start us, length us, event | category | flops | bytes accessed | tf_op | source)
XLA Modules:
  0.0 45.0 jit_solution(17720375876118428764)
XLA Ops:
  0.0 43.4 %shard_map.82 = f32[2,144,128]{2,1,0:T(8,128)} custom-call(f32[2,144,128]{2,1,0:T(8,128)} %bitcast.15, f32[96,96]{1,0:T(8,128)} %ham_ref.1, f32[16,96]{1,0:T(8,128)} %cpl_ref.1, f32[1,16]{1,0:T(1,128)} %bitcast.19, f32[2,16]{1,0:T(2,128)} %strength_ref.1, s32[2,16]{1,0:T(2,128)} %bitcast.16, s32[2,16]{1,0:T(2,128)} %bitcast.17, s32[2,16]{1,0:T(2,128)} %bitcast.18), custom_call_target="tpu_custom_call" | custom-call | tf_op jit(solution)/shard_map/pallas_call | solution.py:288
  43.4 1.6 %copy.12 = f32[1,1,2,2,9216]{4,3,2,1,0:T(2,128)} copy(f32[1,1,2,2,9216]{4,3,2,1,0:T(2,128)} %bitcast.14) | data formatting | bytes 294912
where the time goes:
time: 45.3 us; the launch traced here: 45 us
  Pallas kernels  43.4 us (96%)
  local copies, waits for them, and re-layouts  1.58 us (3%)
    pallas_call x1, Pallas kernels, shards(): pl.pallas_call(kernel, out_shape=jax.ShapeDtypeStruct((2, 144, 128), jnp....  43.4 us
    unnamed x1, local copies, waits for them, and re-layouts  1.58 us

commit v1 on v0

v1 whole, which is shorter than its diff:
```python
import jax
import jax.numpy as jnp
from jax import lax
from jax.experimental import pallas as pl
from jax.experimental.pallas import tpu as pltpu
from jax.sharding import PartitionSpec as P

TIME_STEP = 0.3
STAGES = 4
HIGHEST = lax.Precision.HIGHEST
MESH_ID = pl.DeviceIdType.MESH

LOWER_TIER, UPPER_TIER, LOWER_MODE, UPPER_MODE, LOWER_DIAG, UPPER_DIAG = range(6)
PARTS = 3
SLABS = 9
GROUPS = 24
CUTS = (0, 1, 3, 5, 7, 9)
PIECES = len(CUTS) - 1
LAG = 1


def lane_index():
    return lax.broadcasted_iota(jnp.int32, (GROUPS, 128), 1)


def widen(row):
    lane = lax.broadcasted_iota(jnp.int32, row.shape, 1)
    by96, by64, by32 = (pltpu.roll(row, shift, 1) for shift in (96, 64, 32))
    return (
        jnp.where(lane < 96, row, by96),
        jnp.where(lane < 64, by96, by64),
        jnp.where(lane < 32, by64, by32),
    )


def unpack(parts):
    lane = lane_index()
    first, second, third = parts
    return jnp.concatenate(
        [
            first,
            jnp.where(lane < 32, pltpu.roll(first, 32, 1), pltpu.roll(second, 32, 1)),
            jnp.where(lane < 64, pltpu.roll(second, 64, 1), pltpu.roll(third, 64, 1)),
            pltpu.roll(third, 96, 1),
        ],
        axis=0,
    )


def pack(rows):
    lane = lane_index()
    part = [rows[GROUPS * p : GROUPS * (p + 1)] for p in range(4)]
    one96, two64 = pltpu.roll(part[1], 96, 1), pltpu.roll(part[2], 64, 1)
    return (
        jnp.where(lane < 96, part[0], one96),
        jnp.where(lane < 64, one96, two64),
        jnp.where(lane < 32, two64, pltpu.roll(part[3], 32, 1)),
    )


def kernel(
    a_hbm, ham_hbm, cpl_hbm, rates_hbm, strength_hbm, occ_hbm, up_hbm, down_hbm,
    out_ref,
    a_ref, ham_ref, cpl_ref, rates_ref, strength_ref, occ_ref, up_ref, down_ref, load_sem,
    own, halo, acc, gap_up, gap_down, plus_down, ham_sq, ham_perm, tall, send_sem, recv_sem,
):
    tier, mode = lax.axis_index("tier"), lax.axis_index("mode")
    tiers, modes = lax.axis_size("tier"), lax.axis_size("mode")
    next_mode, prev_mode = lax.rem(mode + 1, modes), lax.rem(mode + modes - 1, modes)
    odd = lax.rem(tier, 2)
    partner = tier + 1 - 2 * odd
    across = lax.rem(tier + 2 * odd + tiers - 1, tiers)
    across_mode = lax.rem(mode + 2 * odd + modes - 1, modes)
    has_across = jnp.logical_and(tier > 0, tier < tiers - 1)

    barrier = pltpu.get_barrier_semaphore()

    def greet(device):
        pl.semaphore_signal(barrier, inc=1, device_id=device, device_id_type=MESH_ID)

    greet((tier, next_mode))
    greet((tier, prev_mode))
    greet((partner, mode))

    @pl.when(has_across)
    def _():
        greet((across, mode))
        greet((across, across_mode))

    loads = [
        pltpu.make_async_copy(src, dst, load_sem.at[i])
        for i, (src, dst) in enumerate(
            zip(
                (a_hbm, ham_hbm, cpl_hbm, rates_hbm, strength_hbm, occ_hbm, up_hbm, down_hbm),
                (a_ref, ham_ref, cpl_ref, rates_ref, strength_ref, occ_ref, up_ref, down_ref),
            )
        )
    ]
    for load in loads:
        load.start()
    loads[0].wait()

    def place(k):
        return k % PARTS, 8 * (k // PARTS)

    for k in range(SLABS):
        u, q = place(k)
        for c in range(4):
            own[0, k, c] = a_ref[c // 2, pl.ds(6 * q + 2 * u + c % 2, 8, stride=6), :]

    @pl.when(has_across)
    def _():
        pl.semaphore_wait(barrier, 5)

    @pl.when(jnp.logical_not(has_across))
    def _():
        pl.semaphore_wait(barrier, 3)

    def copy(n, slot, p, src, device):
        span = pl.ds(CUTS[p], CUTS[p + 1] - CUTS[p])
        return pltpu.make_async_remote_copy(
            src_ref=src.at[span],
            dst_ref=halo.at[n, slot, span],
            send_sem=send_sem.at[n, slot],
            recv_sem=recv_sem.at[n, slot, p],
            device_id=device,
            device_id_type=MESH_ID,
        )

    def arrive(n, slot, p):
        copy(n, slot, p, own.at[n], (partner, mode)).wait_recv()

    def send_own(n, p):
        mine = own.at[n]
        copy(n, LOWER_MODE, p, mine, (tier, next_mode)).start()
        copy(n, UPPER_MODE, p, mine, (tier, prev_mode)).start()

        @pl.when(has_across)
        def _():
            copy(n, UPPER_DIAG - odd, p, mine, (across, across_mode)).start()
            copy(n, UPPER_TIER - odd, p, mine, (across, mode)).start()

        copy(n, LOWER_TIER + odd, p, mine, (partner, mode)).start()

    def relay(n, p):
        copy(n, LOWER_DIAG + odd, p, halo.at[n, LOWER_MODE + odd], (partner, mode)).start()

    for p in range(PIECES):
        send_own(0, p)

    blank = jnp.zeros((4, 8, 128), jnp.float32)

    @pl.when(jnp.logical_not(has_across))
    def _():
        for n in range(STAGES):
            for k in range(SLABS):
                halo[n, LOWER_TIER + odd, k] = blank
                halo[n, LOWER_DIAG + odd, k] = blank

    for load in loads[1:]:
        load.wait()

    raw = ham_ref[...]
    ham_sq[...] = jnp.zeros((128, 128), jnp.float32)
    ham_sq[:96, :96] = 0.5 * (raw + raw.T)
    rows = jnp.concatenate([ham_sq[pl.ds(p, GROUPS, stride=4), :] for p in range(4)], axis=0)
    tall[...] = jnp.concatenate([rows, jnp.zeros((32, 128), jnp.float32)], axis=0).T
    ham_perm[...] = jnp.concatenate([tall[pl.ds(p, GROUPS, stride=4), :] for p in range(4)], axis=0)

    level = occ_ref[...].astype(jnp.float32)
    named = lax.broadcasted_iota(jnp.int32, (8, 16), 0)
    ups, down_re, down_im = [], [], []
    for s in range(2):
        up_mask = (up_ref[s : s + 1, :] == named).astype(jnp.float32)
        down_mask = (down_ref[s : s + 1, :] == named).astype(jnp.float32) * level[s : s + 1, :]
        ups.append(up_mask)
        down_re.append(down_mask * strength_ref[0:1, :])
        down_im.append(down_mask * strength_ref[1:2, :])
    own_rows = lax.broadcasted_iota(jnp.int32, (8, 16), 0) < 2
    down_re = [d + jnp.where(own_rows, v, 0.0) for d, v in zip(down_re, ups)]
    mix = jnp.concatenate(ups + down_re + down_im, axis=0)
    cpl = cpl_ref[...]
    wide_cpl = jnp.concatenate([cpl, jnp.zeros((16, 32), jnp.float32)], axis=1)
    by_lane = jnp.dot(mix, wide_cpl, precision=HIGHEST, preferred_element_type=jnp.float32)
    flat = lax.dot_general(
        wide_cpl, mix, (((0,), (1,)), ((), ())), precision=HIGHEST, preferred_element_type=jnp.float32
    )
    tall[:, :48] = flat
    columns = [tall[pl.ds(p, GROUPS, stride=4), :] for p in range(4)]
    lane = lane_index()
    lanes_wide = widen(by_lane)
    damping = jnp.sum(level * rates_ref[...], axis=1, keepdims=True)
    for e in range(48):
        kind, s, source = e // 16, e // 8 % 2, e % 8
        if kind == 0 and source < 2:
            continue
        spread = [jnp.broadcast_to(columns[p][:, e : e + 1], (GROUPS, 128)) for p in range(4)]
        for u in range(PARTS):
            along_rows = jnp.where(lane < (96, 64, 32)[u], spread[u], spread[u + 1])
            along_lanes = lanes_wide[u][e : e + 1, :]
            if kind == 0:
                gap_up[8 * s + source, u] = along_rows - along_lanes
            elif kind == 1:
                gap_down[8 * s + source, u] = along_rows - along_lanes
            else:
                plus = along_rows + along_lanes
                if source == s:
                    plus = plus - damping[s : s + 1, :]
                plus_down[8 * s + source, u] = plus

    def add_up(sums, src, block, k):
        u, q = place(k)
        for j in range(2):
            real, imag = src[2 * j], src[2 * j + 1]
            for s in range(2):
                gap = gap_up[8 * s + 2 * block + j, u, q : q + 8]
                sums[2 * s] = sums[2 * s] + gap * imag
                sums[2 * s + 1] = sums[2 * s + 1] - gap * real

    def add_down(sums, src, block, k):
        u, q = place(k)
        for j in range(2):
            real, imag = src[2 * j], src[2 * j + 1]
            for s in range(2):
                at = 8 * s + 2 * block + j
                gap, plus = gap_down[at, u, q : q + 8], plus_down[at, u, q : q + 8]
                sums[2 * s] = sums[2 * s] + gap * imag + plus * real
                sums[2 * s + 1] = sums[2 * s + 1] + plus * imag - gap * real

    def local(n):
        whole = [
            unpack([jnp.concatenate([own[n, PARTS * o + u, c] for o in range(3)], axis=0) for u in range(PARTS)])
            for c in range(4)
        ]
        right = jnp.dot(
            jnp.concatenate(whole, axis=0), ham_sq[...], precision=HIGHEST, preferred_element_type=jnp.float32
        )
        left = jnp.dot(
            ham_perm[:, :96], jnp.concatenate(whole, axis=1), precision=HIGHEST, preferred_element_type=jnp.float32
        )
        moved = [pack(left[:, 128 * c : 128 * (c + 1)] - right[96 * c : 96 * (c + 1)]) for c in range(4)]
        for k in range(SLABS):
            u, q = place(k)
            here = [part[u][q : q + 8] for part in moved]
            sums = [here[1], -here[0], here[3], -here[2]]
            add_down(sums, own.at[n, k], 0, k)
            for c in range(4):
                acc[k, c] = sums[c]

    def gather(n, p):
        arrive(n, LOWER_MODE + odd, p)
        relay(n, p)
        arrive(n, UPPER_MODE - odd, p)
        arrive(n, UPPER_TIER - odd, p)

        @pl.when(has_across)
        def _():
            arrive(n, LOWER_TIER + odd, p)

        for k in range(CUTS[p], CUTS[p + 1]):
            sums = [acc[k, c] for c in range(4)]
            add_down(sums, halo.at[n, LOWER_MODE, k], 2, k)
            add_up(sums, halo.at[n, UPPER_MODE, k], 2, k)
            add_down(sums, halo.at[n, LOWER_TIER, k], 1, k)
            add_up(sums, halo.at[n, UPPER_TIER, k], 1, k)
            for c in range(4):
                acc[k, c] = sums[c]

    def finish(n, p):
        arrive(n, UPPER_DIAG - odd, p)

        @pl.when(has_across)
        def _():
            arrive(n, LOWER_DIAG + odd, p)

        for k in range(CUTS[p], CUTS[p + 1]):
            u, q = place(k)
            sums = [acc[k, c] for c in range(4)]
            add_down(sums, halo.at[n, LOWER_DIAG, k], 3, k)
            add_up(sums, halo.at[n, UPPER_DIAG, k], 3, k)
            for c in range(4):
                term = (TIME_STEP / (n + 1)) * sums[c]
                if n < STAGES - 1:
                    own[n + 1, k, c] = term
                else:
                    total = term
                    for back in range(STAGES - 1, -1, -1):
                        total = total + own[back, k, c]
                    out_ref[c // 2, pl.ds(6 * q + 2 * u + c % 2, 8, stride=6), :] = total
        if n < STAGES - 1:
            send_own(n + 1, p)

    for n in range(STAGES):
        local(n)
        for p in range(PIECES + LAG):
            if p < PIECES:
                gather(n, p)
            if p >= LAG:
                finish(n, p - LAG)

    def sent(n, slot):
        pltpu.make_async_remote_copy(
            src_ref=own.at[n],
            dst_ref=halo.at[n, slot],
            send_sem=send_sem.at[n, slot],
            recv_sem=recv_sem.at[n, slot, 0],
            device_id=(partner, mode),
            device_id_type=MESH_ID,
        ).wait_send()

    for n in range(STAGES):
        sent(n, LOWER_MODE)
        sent(n, UPPER_MODE)
        sent(n, LOWER_TIER + odd)
        sent(n, LOWER_DIAG + odd)

        @pl.when(has_across)
        def _():
            sent(n, UPPER_TIER - odd)
            sent(n, UPPER_DIAG - odd)


def shards(ados, hamiltonian, couplings, rates, strength, occupancy, up_index, down_index):
    rows = ados.reshape(2, 2, 72, 128).transpose(0, 2, 1, 3).reshape(2, 144, 128)
    operands = (
        rows, hamiltonian, couplings, rates.reshape(1, -1), strength,
        occupancy.reshape(2, -1), up_index.reshape(2, -1), down_index.reshape(2, -1),
    )
    real = jnp.float32
    done = pl.pallas_call(
        kernel,
        out_shape=jax.ShapeDtypeStruct((2, 144, 128), real),
        in_specs=[pl.BlockSpec(memory_space=pl.ANY)] * 8,
        out_specs=pl.BlockSpec(memory_space=pltpu.VMEM),
        scratch_shapes=[pltpu.VMEM(x.shape, x.dtype) for x in operands] + [
            pltpu.SemaphoreType.DMA((8,)),
            pltpu.VMEM((STAGES, SLABS, 4, 8, 128), real),
            pltpu.VMEM((STAGES, 6, SLABS, 4, 8, 128), real),
            pltpu.VMEM((SLABS, 4, 8, 128), real),
            pltpu.VMEM((16, PARTS, GROUPS, 128), real),
            pltpu.VMEM((16, PARTS, GROUPS, 128), real),
            pltpu.VMEM((16, PARTS, GROUPS, 128), real),
            pltpu.VMEM((128, 128), real),
            pltpu.VMEM((96, 128), real),
            pltpu.VMEM((128, 128), real),
            pltpu.SemaphoreType.DMA((STAGES, 6)),
            pltpu.SemaphoreType.DMA((STAGES, 6, PIECES)),
        ],
        compiler_params=pltpu.CompilerParams(collective_id=0, has_side_effects=True),
    )(*operands)
    return done.reshape(2, 72, 2, 128).transpose(0, 2, 1, 3).reshape(ados.shape)


def solution(mesh):
    split = P("tier", "mode", None, None)
    in_specs = (P("tier", "mode", None, None, None), P(), P(), P(), P(), split, split, split)
    out_specs = P("tier", "mode", None, None, None)
    return jax.shard_map(shards, mesh=mesh, in_specs=in_specs, out_specs=out_specs, check_vma=False)
```

time: 45.3 us -> 38.7 us (0.85)
  Pallas kernels: 43.4 us -> 37 us
    pallas_call x1, Pallas kernels: 43.4 us -> 37 us  [shards(): pl.pallas_call(kernel, out_shape=jax.ShapeDtypeStruct((2, 144, 128), real...]
where the time goes in v1:
time: 38.7 us; the launch traced here: 38.6 us
  Pallas kernels  37 us (96%)
  local copies, waits for them, and re-layouts  1.58 us (4%)
    pallas_call x1, Pallas kernels, shards(): pl.pallas_call(kernel, out_shape=jax.ShapeDtypeStruct((2, 144, 128), real...  37 us
    unnamed x1, local copies, waits for them, and re-layouts  1.58 us

profile of v1, /device:TPU:1, one launch (start us, length us, event | category | flops | bytes accessed | tf_op | source)
XLA Modules:
  0.0 38.6 jit_solution(12249371352694276385)
XLA Ops:
  0.0 37.0 %shard_map.82 = f32[2,144,128]{2,1,0:T(8,128)} custom-call(f32[2,144,128]{2,1,0:T(8,128)} %bitcast.15, f32[96,96]{1,0:T(8,128)} %ham_hbm.1, f32[16,96]{1,0:T(8,128)} %cpl_hbm.1, f32[1,16]{1,0:T(1,128)} %bitcast.19, f32[2,16]{1,0:T(2,128)} %strength_hbm.1, s32[2,16]{1,0:T(2,128)} %bitcast.16, s32[2,16]{1,0:T(2,128)} %bitcast.17, s32[2,16]{1,0:T(2,128)} %bitcast.18), custom_call_target="tpu_custom_call" | custom-call | tf_op jit(solution)/shard_map/pallas_call | solution.py:330
  37.0 1.6 %copy.12 = f32[1,1,2,2,9216]{4,3,2,1,0:T(2,128)} copy(f32[1,1,2,2,9216]{4,3,2,1,0:T(2,128)} %bitcast.14) | data formatting | bytes 294912

commit v2 on v1

--- a/solution.py
+++ b/solution.py
@@ -327,10 +327,11 @@
         occupancy.reshape(2, -1), up_index.reshape(2, -1), down_index.reshape(2, -1),
     )
     real = jnp.float32
+    operands = [pltpu.with_memory_space_constraint(x, pltpu.HBM) for x in operands]
     done = pl.pallas_call(
         kernel,
         out_shape=jax.ShapeDtypeStruct((2, 144, 128), real),
-        in_specs=[pl.BlockSpec(memory_space=pl.ANY)] * 8,
+        in_specs=[pl.BlockSpec(memory_space=pltpu.HBM)] * 8,
         out_specs=pl.BlockSpec(memory_space=pltpu.VMEM),
         scratch_shapes=[pltpu.VMEM(x.shape, x.dtype) for x in operands] + [
             pltpu.SemaphoreType.DMA((8,)),
@@ -346,7 +347,7 @@
             pltpu.SemaphoreType.DMA((STAGES, 6)),
             pltpu.SemaphoreType.DMA((STAGES, 6, PIECES)),
         ],
-        compiler_params=pltpu.CompilerParams(collective_id=0, has_side_effects=True),
+        compiler_params=pltpu.CompilerParams(collective_id=0, has_side_effects=True, vmem_limit_bytes=16 * 2**20),
     )(*operands)
     return done.reshape(2, 72, 2, 128).transpose(0, 2, 1, 3).reshape(ados.shape)
 

time: 38.7 us -> 37.1 us (0.959)
  local copies, waits for them, and re-layouts: 1.58 us -> 0.66 us
  Pallas kernels: 37 us -> 36.3 us
    unnamed x1, local copies, waits for them, and re-layouts: 1.58 us -> 0.66 us
    pallas_call x1, Pallas kernels: 37 us -> 36.3 us  [shards(): pl.pallas_call(kernel, out_shape=jax.ShapeDtypeStruct((2, 144, 128), real...]
where the time goes in v2:
time: 37.1 us; the launch traced here: 37 us
  Pallas kernels  36.3 us (98%)
  local copies, waits for them, and re-layouts  0.66 us (2%)
    pallas_call x1, Pallas kernels, shards(): pl.pallas_call(kernel, out_shape=jax.ShapeDtypeStruct((2, 144, 128), real...  36.3 us

profile of v2, /device:TPU:1, one launch (start us, length us, event | category | flops | bytes accessed | tf_op | source)
XLA Modules:
  0.0 37.0 jit_solution(12443875808247087326)
XLA Ops:
  0.0 36.3 %shard_map.82 = f32[2,144,128]{2,1,0:T(8,128)S(1)} custom-call(f32[2,144,128]{2,1,0:T(8,128)} %bitcast.15, f32[96,96]{1,0:T(8,128)} %ham_hbm.1, f32[16,96]{1,0:T(8,128)} %cpl_hbm.1, f32[1,16]{1,0:T(1,128)} %bitcast.19, f32[2,16]{1,0:T(2,128)} %strength_hbm.1, s32[2,16]{1,0:T(2,128)} %bitcast.16, s32[2,16]{1,0:T(2,128)} %bitcast.17, s32[2,16]{1,0:T(2,128)} %bitcast.18), custom_call_target="tpu_custom_call" | custom-call | tf_op jit(solution)/shard_map/pallas_call | solution.py:331
  36.4 0.7 %copy.12 = f32[1,1,2,2,9216]{4,3,2,1,0:T(2,128)} copy(f32[1,1,2,2,9216]{4,3,2,1,0:T(2,128)S(1)} %bitcast.14) | data formatting | bytes 294912

commit v3 on v2

--- a/solution.py
+++ b/solution.py
@@ -16,7 +16,6 @@
 GROUPS = 24
 CUTS = (0, 1, 3, 5, 7, 9)
 PIECES = len(CUTS) - 1
-LAG = 1
 
 
 def lane_index():
@@ -69,6 +68,7 @@
     next_mode, prev_mode = lax.rem(mode + 1, modes), lax.rem(mode + modes - 1, modes)
     odd = lax.rem(tier, 2)
     partner = tier + 1 - 2 * odd
+    near_mode = lax.rem(mode + modes + 1 - 2 * odd, modes)
     across = lax.rem(tier + 2 * odd + tiers - 1, tiers)
     across_mode = lax.rem(mode + 2 * odd + modes - 1, modes)
     has_across = jnp.logical_and(tier > 0, tier < tiers - 1)
@@ -132,12 +132,16 @@
 
     def send_own(n, p):
         mine = own.at[n]
-        copy(n, LOWER_MODE, p, mine, (tier, next_mode)).start()
-        copy(n, UPPER_MODE, p, mine, (tier, prev_mode)).start()
+        copy(n, LOWER_MODE + odd, p, mine, (tier, near_mode)).start()
 
         @pl.when(has_across)
         def _():
             copy(n, UPPER_DIAG - odd, p, mine, (across, across_mode)).start()
+
+        copy(n, UPPER_MODE - odd, p, mine, (tier, across_mode)).start()
+
+        @pl.when(has_across)
+        def _():
             copy(n, UPPER_TIER - odd, p, mine, (across, mode)).start()
 
         copy(n, LOWER_TIER + odd, p, mine, (partner, mode)).start()
@@ -247,9 +251,11 @@
             for c in range(4):
                 acc[k, c] = sums[c]
 
-    def gather(n, p):
+    def pass_on(n, p):
         arrive(n, LOWER_MODE + odd, p)
         relay(n, p)
+
+    def gather(n, p):
         arrive(n, UPPER_MODE - odd, p)
         arrive(n, UPPER_TIER - odd, p)
 
@@ -292,11 +298,12 @@
 
     for n in range(STAGES):
         local(n)
-        for p in range(PIECES + LAG):
-            if p < PIECES:
-                gather(n, p)
-            if p >= LAG:
-                finish(n, p - LAG)
+        pass_on(n, 0)
+        for p in range(PIECES):
+            gather(n, p)
+            if p + 1 < PIECES:
+                pass_on(n, p + 1)
+            finish(n, p)
 
     def sent(n, slot):
         pltpu.make_async_remote_copy(

time: 37.1 us -> 36.4 us (0.981)
  Pallas kernels: 36.3 us -> 35.7 us
    pallas_call x1, Pallas kernels: 36.3 us -> 35.7 us  [shards(): pl.pallas_call(kernel, out_shape=jax.ShapeDtypeStruct((2, 144, 128), real...]
where the time goes in v3:
time: 36.4 us
  Pallas kernels  35.7 us (98%)
  local copies, waits for them, and re-layouts  0.66 us (2%)
    pallas_call x1, Pallas kernels, shards(): pl.pallas_call(kernel, out_shape=jax.ShapeDtypeStruct((2, 144, 128), real...  35.7 us

profile of v3, /device:TPU:1, one launch (start us, length us, event | category | flops | bytes accessed | tf_op | source)
XLA Modules:
  0.0 36.4 jit_solution(6539946015693198357)
XLA Ops:
  0.0 35.7 %shard_map.82 = f32[2,144,128]{2,1,0:T(8,128)S(1)} custom-call(f32[2,144,128]{2,1,0:T(8,128)} %bitcast.15, f32[96,96]{1,0:T(8,128)} %ham_hbm.1, f32[16,96]{1,0:T(8,128)} %cpl_hbm.1, f32[1,16]{1,0:T(1,128)} %bitcast.19, f32[2,16]{1,0:T(2,128)} %strength_hbm.1, s32[2,16]{1,0:T(2,128)} %bitcast.16, s32[2,16]{1,0:T(2,128)} %bitcast.17, s32[2,16]{1,0:T(2,128)} %bitcast.18), custom_call_target="tpu_custom_call" | custom-call | tf_op jit(solution)/shard_map/pallas_call | solution.py:338
  35.7 0.7 %copy.12 = f32[1,1,2,2,9216]{4,3,2,1,0:T(2,128)} copy(f32[1,1,2,2,9216]{4,3,2,1,0:T(2,128)S(1)} %bitcast.14) | data formatting | bytes 294912

commit v4 on v3

--- a/solution.py
+++ b/solution.py
@@ -137,12 +137,9 @@
         @pl.when(has_across)
         def _():
             copy(n, UPPER_DIAG - odd, p, mine, (across, across_mode)).start()
+            copy(n, UPPER_TIER - odd, p, mine, (across, mode)).start()
 
         copy(n, UPPER_MODE - odd, p, mine, (tier, across_mode)).start()
-
-        @pl.when(has_across)
-        def _():
-            copy(n, UPPER_TIER - odd, p, mine, (across, mode)).start()
 
         copy(n, LOWER_TIER + odd, p, mine, (partner, mode)).start()
 
@@ -296,15 +293,6 @@
         if n < STAGES - 1:
             send_own(n + 1, p)
 
-    for n in range(STAGES):
-        local(n)
-        pass_on(n, 0)
-        for p in range(PIECES):
-            gather(n, p)
-            if p + 1 < PIECES:
-                pass_on(n, p + 1)
-            finish(n, p)
-
     def sent(n, slot):
         pltpu.make_async_remote_copy(
             src_ref=own.at[n],
@@ -315,7 +303,7 @@
             device_id_type=MESH_ID,
         ).wait_send()
 
-    for n in range(STAGES):
+    def all_sent(n):
         sent(n, LOWER_MODE)
         sent(n, UPPER_MODE)
         sent(n, LOWER_TIER + odd)
@@ -325,6 +313,19 @@
         def _():
             sent(n, UPPER_TIER - odd)
             sent(n, UPPER_DIAG - odd)
+
+    for n in range(STAGES):
+        local(n)
+        pass_on(n, 0)
+        for p in range(PIECES):
+            gather(n, p)
+            if p + 1 < PIECES:
+                pass_on(n, p + 1)
+            finish(n, p)
+            if p == PIECES - 2 and n > 0:
+                all_sent(n - 1)
+
+    all_sent(STAGES - 1)
 
 
 def shards(ados, hamiltonian, couplings, rates, strength, occupancy, up_index, down_index):

time: 36.4 us -> 36.4 us (level)
  no operation moved by 1% of the time
where the time goes in v4:
time: 36.4 us; the launch traced here: 36.3 us
  Pallas kernels  35.7 us (98%)
  local copies, waits for them, and re-layouts  0.66 us (2%)
    pallas_call x1, Pallas kernels, shards(): pl.pallas_call(kernel, out_shape=jax.ShapeDtypeStruct((2, 144, 128), real...  35.7 us

profile of v4, /device:TPU:1, one launch (start us, length us, event | category | flops | bytes accessed | tf_op | source)
XLA Modules:
  0.0 36.3 jit_solution(14307459786688769642)
XLA Ops:
  0.0 35.7 %shard_map.82 = f32[2,144,128]{2,1,0:T(8,128)S(1)} custom-call(f32[2,144,128]{2,1,0:T(8,128)} %bitcast.15, f32[96,96]{1,0:T(8,128)} %ham_hbm.1, f32[16,96]{1,0:T(8,128)} %cpl_hbm.1, f32[1,16]{1,0:T(1,128)} %bitcast.19, f32[2,16]{1,0:T(2,128)} %strength_hbm.1, s32[2,16]{1,0:T(2,128)} %bitcast.16, s32[2,16]{1,0:T(2,128)} %bitcast.17, s32[2,16]{1,0:T(2,128)} %bitcast.18), custom_call_target="tpu_custom_call" | custom-call | tf_op jit(solution)/shard_map/pallas_call | solution.py:339
  35.7 0.7 %copy.12 = f32[1,1,2,2,9216]{4,3,2,1,0:T(2,128)} copy(f32[1,1,2,2,9216]{4,3,2,1,0:T(2,128)S(1)} %bitcast.14) | data formatting | bytes 294912
